TPU v7x, 32 devices: a whole 2x2x4 slice. The times are simulated.
32 devices in a mesh: vocab: 8 (over z, x), batch: 4 (over y, core).
Axes of the slice: x: 2, y: 2, z: 4, core: 2. Of those that a mesh axis runs over, the one named last changes fastest.
Arguments:
- hidden: bfloat16 [256, 1024], P(('vocab', 'batch'))
- embedding: bfloat16 [8192, 1024], P('vocab')
- block_counts: int32 [64], P('vocab'), may hold values from 1 to 4095
- lang_blocks: int32 [200, 64], replicated, may hold values from -1 to 63, as said below
- sent_lang: int32 [4], replicated, may hold values from 0 to 199
- targets: int32 [256], replicated, may hold values from 0 to 8191, as said below
Outputs:
- token_loss: float32 [256], P(('vocab', 'batch'))
- grad_embed: bfloat16 [8192, 1024], P(('vocab', 'batch'))
Inputs may be any that keep to these rules, and one draw needn't show every extreme that they name: `lang_blocks`: each list holds distinct block numbers and then -1 padding; the first entry of every list is block 0; at least 16 entries are blocks, and some language fills all 64 entries. `targets`: the target of token t lies in a block listed for the language of sentence t // 64.
All inputs are finite; a program needn't handle non-finite values.
Results may differ from a plain program's by a relative error of at most 0.0075.
Values may be sent and summed in bfloat16 or wider, within the bound.
No kernel may reach another device: no remote copies, remote signals or barrier semaphores. Data moves between devices by JAX's collectives and lax.ppermute only.
A program may use at most 64 MiB of HBM per device.

v0:
```python
import jax
import jax.numpy as jnp
from jax import lax
from jax.sharding import PartitionSpec as P

SEQ = 64
masked_fill = -1e30


def body(hidden, embedding, block_counts, lang_blocks, sent_lang, targets):
    tok_dev = hidden.shape[0]
    vocab_count = lax.axis_size("vocab")
    batch_count = lax.axis_size("batch")
    vocab_index = lax.axis_index("vocab")
    batch_index = lax.axis_index("batch")
    local_rows = embedding.shape[0]
    local_blocks = block_counts.shape[0]
    block_width = local_rows // local_blocks
    gathered = lax.all_gather(hidden, "vocab", axis=0, tiled=True)
    token_count = gathered.shape[0]
    token_ids = (
        (jnp.arange(vocab_count, dtype=jnp.int32)[:, None] * batch_count + batch_index) * tok_dev
        + jnp.arange(tok_dev, dtype=jnp.int32)[None, :]
    ).reshape(-1)
    target_ids = lax.dynamic_index_in_dim(
        targets.reshape(vocab_count, batch_count, tok_dev), batch_index, 1, keepdims=False
    ).reshape(-1)
    sentence = token_ids // SEQ
    sentence_hit = sentence[:, None] == jnp.arange(sent_lang.shape[0], dtype=jnp.int32)[None, :]
    token_language = jnp.sum(jnp.where(sentence_hit, sent_lang[None, :], 0), axis=1)
    block_ids = vocab_index * local_blocks + jnp.arange(local_blocks, dtype=jnp.int32)
    member = jnp.any(lang_blocks[:, :, None] == block_ids[None, None, :], axis=1).astype(
        jnp.float32
    )
    language_hit = (
        token_language[:, None] == jnp.arange(lang_blocks.shape[0], dtype=jnp.int32)[None, :]
    ).astype(jnp.float32)
    allowed = jnp.dot(language_hit, member, precision=lax.Precision.HIGHEST) > 0.5
    allowed_cells = allowed[:, :, None]
    raw_scores = lax.dot_general(
        gathered, embedding, (((1,), (1,)), ((), ())), preferred_element_type=jnp.float32
    )
    log_sampling = jnp.log(block_counts.astype(jnp.float32))
    logits = (
        raw_scores.reshape(token_count, local_blocks, block_width) - log_sampling[None, :, None]
    )
    masked = jnp.where(allowed_cells, logits, masked_fill)
    word_ids = (vocab_index * local_rows + jnp.arange(local_rows, dtype=jnp.int32)).reshape(
        local_blocks, block_width
    )
    is_target = word_ids[None, :, :] == target_ids[:, None, None]
    local_peak = jnp.max(masked, axis=(1, 2))
    local_target = jnp.sum(jnp.where(is_target, logits, 0.0), axis=(1, 2))
    peak_value = lax.pmax(local_peak, "vocab")
    local_total = jnp.sum(
        jnp.where(allowed_cells, jnp.exp(masked - peak_value[:, None, None]), 0.0), axis=(1, 2)
    )
    denominator, target_logit = lax.psum((local_total, local_target), "vocab")
    log_total = peak_value + jnp.log(denominator)
    every_loss = log_total - target_logit
    token_loss = lax.dynamic_slice_in_dim(every_loss, vocab_index * tok_dev, tok_dev, 0)
    softmax_weights = jnp.where(allowed_cells, jnp.exp(logits - log_total[:, None, None]), 0.0)
    grad_logits = (
        (softmax_weights - is_target.astype(jnp.float32))
        .astype(jnp.bfloat16)
        .reshape(token_count, local_rows)
    )
    columns = lax.all_to_all(grad_logits, "batch", split_axis=1, concat_axis=0, tiled=True)
    everyone = lax.all_gather(gathered, "batch", axis=0, tiled=True)
    summed = jnp.zeros((columns.shape[1], gathered.shape[1]), jnp.float32)
    for source in range(batch_count):
        slice_grad = columns[source * token_count : (source + 1) * token_count]
        slice_rows = everyone[source * token_count : (source + 1) * token_count]
        contribution = lax.dot_general(
            slice_grad, slice_rows, (((0,), (0,)), ((), ())), preferred_element_type=jnp.float32
        )
        rounded = lax.optimization_barrier(contribution.astype(jnp.bfloat16))
        summed = summed + rounded.astype(jnp.float32)
    grad_embed = summed.astype(jnp.bfloat16)
    return (token_loss, grad_embed)


def solution(mesh):
    in_specs = (P(("vocab", "batch"), None), P("vocab", None), P("vocab"), P(), P(), P())
    out_specs = (P(("vocab", "batch")), P(("vocab", "batch"), None))
    return jax.shard_map(body, mesh=mesh, in_specs=in_specs, out_specs=out_specs, check_vma=False)
```

profile of v0, /device:TPU:0, one launch (start us, length us, event | category | flops | bytes accessed | tf_op | source)
XLA Modules:
  0.0 92.3 jit_solution(3741572874803002125)
XLA Ops:
  0.6 0.0 copy-start
  0.7 0.8 convert_log_fusion
  1.5 0.1 broadcast_bitcast_fusion
  1.6 0.1 iota_add_fusion
  1.6 0.1 add.93
  1.7 1.0 %compare_reduce_fusion = pred[200,8]{0,1:T(8,128)(4,1)S(1)} fusion(s32[200,64]{0,1:T(8,128)} %param.9, s32[8]{0:T(128)S(1)} %iota_add_fusion.1), kind=kLoop, calls=%fused_computation.7 | loop fusion | flops 203200 | bytes 52832 | tf_op jit(solution)/shard_map/reduce_or | solution.py:32
  2.7 0.7 select_reduce_fusion.1
  3.5 0.2 convolution_compare_fusion
  3.7 0.1 copy.13
  3.8 0.8 reshape.91
  4.6 0.1 eq.66
  4.7 32.5 %all_gather.6 = bf16[64,1024]{1,0:T(8,128)(2,1)S(1)} all-gather(bf16[8,1024]{1,0:T(8,128)(2,1)} %param.6), channel_id=1, replica_groups=mesh['vocab'=8,'batch'=4] {'vocab'}, dimensions={0}, use_global_device_ids=true | all-gather | bytes 147456 | tf_op jit(solution)/shard_map/all_gather | solution.py:19
  37.2 0.1 broadcast_in_dim.53
  37.3 0.0 copy-done
  37.3 0.9 fusion.3
  38.2 21.3 %pmax.7 = f32[64]{0:T(128)S(1)} all-reduce(f32[64]{0:T(128)S(1)} %get-tuple-element.8), channel_id=1, replica_groups=mesh['vocab'=8,'batch'=4] {'vocab'}, use_global_device_ids=true, to_apply=%region_3.4 | all-reduce | flops 64 | bytes 512 | tf_op jit(solution)/shard_map/pmax | solution.py:54
  59.5 0.3 fusion
  59.8 17.1 %all-reduce = (f32[64]{0:T(128)S(1)}, f32[64]{0:T(128)S(1)}) all-reduce(f32[64]{0:T(128)S(1)} %get-tuple-element.3, f32[64]{0:T(128)S(1)} %get-tuple-element.2), channel_id=1, replica_groups=mesh['vocab'=8,'batch'=4] {'vocab'}, use_global_device_ids=true, to_apply=%region_5.6 | all-reduce | flops 128 | bytes 1024 | tf_op jit(solution)/shard_map/psum | solution.py:58
  76.9 0.1 fusion.2
  77.1 0.7 copy.21
  77.7 3.3 %all-to-all-start = ((bf16[64,4,256]{2,0,1:T(8,128)(2,1)}), bf16[64,4,256]{2,0,1:T(8,128)(2,1)S(1)}, u32[]{:S(2)}, u32[]{:S(2)}) async-start(bf16[64,4,256]{2,0,1:T(8,128)(2,1)} %bitcast.32), calls=%async_computation | async-start | bytes 262144 | tf_op jit(solution)/shard_map/all_to_all | solution.py:68
  81.1 8.2 %all_gather.7 = bf16[256,1024]{1,0:T(8,128)(2,1)S(1)} all-gather(bf16[64,1024]{1,0:T(8,128)(2,1)S(1)} %all_gather.6), channel_id=1, replica_groups=mesh['vocab'=8,'batch'=4] {'batch'}, dimensions={0}, use_global_device_ids=true | all-gather | bytes 655360 | tf_op jit(solution)/shard_map/all_gather | solution.py:69
  89.3 0.6 dynamic_slice.8
  89.9 0.0 all-to-all-done
  89.9 0.3 convolution_convert_fusion
  90.2 0.3 convolution_convert_fusion.1
  90.5 0.3 convolution_convert_fusion.2
  90.9 0.3 convolution_convert_fusion.3
  91.2 1.1 %add_convert_fusion = bf16[256,1024]{1,0:T(8,128)(2,1)} fusion(bf16[256,1024]{1,0:T(8,128)(2,1)S(1)} %convolution_convert_fusion, bf16[256,1024]{1,0:T(8,128)(2,1)S(1)} %convolution_convert_fusion.1, bf16[256,1024]{1,0:T(8,128)(2,1)S(1)} %convolution_convert_fusion.2, bf16[256,1024]{1,0:T(8,128)(2,1)S(1)} %convolution_convert_fusion.3), kind=kLoop, calls=%fused_computation.6 | loop fusion | flops 2097152 | bytes 2621440 | tf_op jit(solution)/shard_map/convert_element_type | solution.py:79
  (6 shorter events, 0.1 us)
Async XLA Ops:
  0.6 36.7 %copy-start = (bf16[1024,1024]{1,0:T(8,128)(2,1)S(1)}, bf16[1024,1024]{1,0:T(8,128)(2,1)}, u32[]{:S(2)}) copy-start(bf16[1024,1024]{1,0:T(8,128)(2,1)} %param.7) | copy-start | bytes 6291460
  77.7 12.2 %all-to-all-start = ((bf16[64,4,256]{2,0,1:T(8,128)(2,1)}), bf16[64,4,256]{2,0,1:T(8,128)(2,1)S(1)}, u32[]{:S(2)}, u32[]{:S(2)}) async-start(bf16[64,4,256]{2,0,1:T(8,128)(2,1)} %bitcast.32), calls=%async_computation | async-start | bytes 262144 | tf_op jit(solution)/shard_map/all_to_all | solution.py:68
where the time goes:
time: 92.7 us; the launch traced here: 92.3 us
  blocking collectives  79.2 us (85%)
  other arithmetic  4.2 us (5%)
  starting transfers between devices  3.33 us (4%)
  local copies, waits for them, and re-layouts  2.52 us (3%)
  matrix products  2.32 us (3%)
    all_gather x1, blocking collectives, body(): gathered = lax.all_gather(hidden, 'vocab', axis=0, tiled=True)  32.5 us
    pmax x1, blocking collectives, body(): peak_value = lax.pmax(local_peak, 'vocab')  21.3 us
    psum x1, blocking collectives, body(): denominator, target_logit = lax.psum((local_total, local_target), 'vocab')  17.1 us
    all_gather x1, blocking collectives, body(): everyone = lax.all_gather(gathered, 'batch', axis=0, tiled=True)  8.24 us
    all_to_all x1, starting transfers between devices, body(): lax.all_to_all(grad_logits, 'batch', split_axis=1, concat_axis=0, tiled=T...  3.33 us
  transfers between devices with their start and end apart: 1, of which 0 were waited for; matrix products, arithmetic and copies ran while one was open for 1% of the time, Pallas kernels for 0%

commit v1 on v0

--- a/solution.py
+++ b/solution.py
@@ -16,7 +16,15 @@
     local_rows = embedding.shape[0]
     local_blocks = block_counts.shape[0]
     block_width = local_rows // local_blocks
-    gathered = lax.all_gather(hidden, "vocab", axis=0, tiled=True)
+    last, current_arr, out_arr = (lax.axis_size("vocab"), lax.axis_index("vocab"), hidden.shape[0])
+    views = [(ix, (ix + 1) % last) for ix in range(last)]
+    gathered = jnp.zeros((*hidden.shape[:0], last * out_arr, *hidden.shape[1:]), hidden.dtype)
+    shaped = hidden
+    for u in range(last):
+        seen_now = (current_arr - u) % last
+        gathered = lax.dynamic_update_slice_in_dim(gathered, shaped, seen_now * out_arr, axis=0)
+        if u < last - 1:
+            shaped = lax.ppermute(shaped, "vocab", views)
     token_count = gathered.shape[0]
     token_ids = (
         (jnp.arange(vocab_count, dtype=jnp.int32)[:, None] * batch_count + batch_index) * tok_dev

time: 92.7 us -> 101 us (1.090)
  waiting for transfers between devices: 0.01 us -> 37.8 us
  blocking collectives: 79.2 us -> 44.5 us
  starting transfers between devices: 3.33 us -> 7.58 us
    ppermute x0 -> x7, waiting for transfers between devices: none -> 37.8 us  [body(): shaped = lax.ppermute(shaped, 'vocab', views)]
    all_gather x1 -> x0, blocking collectives: 32.5 us -> none  [body(): gathered = lax.all_gather(hidden, 'vocab', axis=0, tiled=True)]
    ppermute x0 -> x7, starting transfers between devices: none -> 4.26 us  [body(): shaped = lax.ppermute(shaped, 'vocab', views)]
    pmax x1, blocking collectives: 21.3 us -> 17.1 us  [body(): peak_value = lax.pmax(local_peak, 'vocab')]
    psum x1, blocking collectives: 17.1 us -> 19.1 us  [body(): denominator, target_logit = lax.psum((local_total, local_target), 'vocab')]
  transfers between devices with their start and end apart: 1 -> 8, of which waited for: 0 -> 7; matrix products, arithmetic and copies ran while one was open for 1% -> 5% of each run, Pallas kernels for 0% -> 0%
where the time goes in v1:
time: 101 us; the launch traced here: 100 us
  blocking collectives  44.5 us (44%)
  waiting for transfers between devices  37.8 us (37%)
  starting transfers between devices  7.58 us (8%)
  other arithmetic  4.05 us (4%)
  local copies, waits for them, and re-layouts  3.27 us (3%)
  matrix products  2.31 us (2%)
    ppermute x7, waiting for transfers between devices, body(): shaped = lax.ppermute(shaped, 'vocab', views)  37.8 us
    psum x1, blocking collectives, body(): denominator, target_logit = lax.psum((local_total, local_target), 'vocab')  19.1 us
    pmax x1, blocking collectives, body(): peak_value = lax.pmax(local_peak, 'vocab')  17.1 us
    all_gather x1, blocking collectives, body(): everyone = lax.all_gather(gathered, 'batch', axis=0, tiled=True)  8.24 us
    ppermute x7, starting transfers between devices, body(): shaped = lax.ppermute(shaped, 'vocab', views)  4.26 us
    all_to_all x1, starting transfers between devices, body(): lax.all_to_all(grad_logits, 'batch', split_axis=1, concat_axis=0, tiled=T...  3.33 us
  transfers between devices with their start and end apart: 8, of which 7 were waited for; matrix products, arithmetic and copies ran while one was open for 5% of the time, Pallas kernels for 0%

profile of v1, /device:TPU:0, one launch (start us, length us, event | category | flops | bytes accessed | tf_op | source)
XLA Modules:
  0.0 100.3 jit_solution(8459681493124986939)
XLA Ops:
  0.6 3.0 %collective-permute-start = (bf16[8,1024]{1,0:T(8,128)(2,1)}, bf16[8,1024]{1,0:T(8,128)(2,1)S(1)}, u32[]{:S(2)}, u32[]{:S(2)}) collective-permute-start(bf16[8,1024]{1,0:T(8,128)(2,1)} %param.6), channel_id=1, source_target_pairs={{0,4},{4,8},{8,12},{12,16},{16,20},{20,24},{24,28},{28,0},{1,5},{5... | collective-permute-start | bytes 49160 | tf_op jit(solution)/shard_map/ppermute | solution.py:27
  3.7 0.7 convert_log_fusion
  4.5 0.1 add.149
  4.6 1.0 compare_reduce_fusion
  5.6 0.7 select_reduce_fusion.1
  6.3 0.2 convolution_compare_fusion
  6.5 0.7 constant_dynamic-update-slice_fusion.7
  7.3 0.1 copy.13
  7.4 0.8 reshape.91
  8.3 0.4 collective-permute-done
  8.6 1.2 %collective-permute-start.1 = (bf16[8,1024]{1,0:T(8,128)(2,1)S(1)}, bf16[8,1024]{1,0:T(8,128)(2,1)S(1)}, u32[]{:S(2)}, u32[]{:S(2)}) collective-permute-start(bf16[8,1024]{1,0:T(8,128)(2,1)S(1)} %collective-permute-done), channel_id=1, source_target_pairs={{0,4},{4,8},{8,12},{12,16},{16,20},{20,24},{24,28},{28,0},{1,5},{5... | collective-permute-start | bytes 49160 | tf_op jit(solution)/shard_map/ppermute | solution.py:27
  9.9 5.2 %collective-permute-done.1 = bf16[8,1024]{1,0:T(8,128)(2,1)S(1)} collective-permute-done((bf16[8,1024]{1,0:T(8,128)(2,1)S(1)}, bf16[8,1024]{1,0:T(8,128)(2,1)S(1)}, u32[]{:S(2)}, u32[]{:S(2)}) %collective-permute-start.1) | collective-permute-done | bytes 16416 | tf_op jit(solution)/shard_map/ppermute | solution.py:27
  15.1 6.4 %collective-permute-done.2 = bf16[8,1024]{1,0:T(8,128)(2,1)S(1)} collective-permute-done((bf16[8,1024]{1,0:T(8,128)(2,1)S(1)}, bf16[8,1024]{1,0:T(8,128)(2,1)S(1)}, u32[]{:S(2)}, u32[]{:S(2)}) %collective-permute-start.2) | collective-permute-done | bytes 16416 | tf_op jit(solution)/shard_map/ppermute | solution.py:27
  21.5 6.4 %collective-permute-done.3 = bf16[8,1024]{1,0:T(8,128)(2,1)S(1)} collective-permute-done((bf16[8,1024]{1,0:T(8,128)(2,1)S(1)}, bf16[8,1024]{1,0:T(8,128)(2,1)S(1)}, u32[]{:S(2)}, u32[]{:S(2)}) %collective-permute-start.3) | collective-permute-done | bytes 16416 | tf_op jit(solution)/shard_map/ppermute | solution.py:27
  27.9 6.5 %collective-permute-done.4 = bf16[8,1024]{1,0:T(8,128)(2,1)S(1)} collective-permute-done((bf16[8,1024]{1,0:T(8,128)(2,1)S(1)}, bf16[8,1024]{1,0:T(8,128)(2,1)S(1)}, u32[]{:S(2)}, u32[]{:S(2)}) %collective-permute-start.4) | collective-permute-done | bytes 16416 | tf_op jit(solution)/shard_map/ppermute | solution.py:27
  34.5 6.4 %collective-permute-done.5 = bf16[8,1024]{1,0:T(8,128)(2,1)S(1)} collective-permute-done((bf16[8,1024]{1,0:T(8,128)(2,1)S(1)}, bf16[8,1024]{1,0:T(8,128)(2,1)S(1)}, u32[]{:S(2)}, u32[]{:S(2)}) %collective-permute-start.5) | collective-permute-done | bytes 16416 | tf_op jit(solution)/shard_map/ppermute | solution.py:27
  40.9 6.4 %collective-permute-done.6 = bf16[8,1024]{1,0:T(8,128)(2,1)S(1)} collective-permute-done((bf16[8,1024]{1,0:T(8,128)(2,1)S(1)}, bf16[8,1024]{1,0:T(8,128)(2,1)S(1)}, u32[]{:S(2)}, u32[]{:S(2)}) %collective-permute-start.6) | collective-permute-done | bytes 16416 | tf_op jit(solution)/shard_map/ppermute | solution.py:27
  47.3 0.1 broadcast_in_dim.56
  47.5 0.9 fusion.3
  48.3 17.1 %pmax.7 = f32[64]{0:T(128)S(1)} all-reduce(f32[64]{0:T(128)S(1)} %get-tuple-element.8), channel_id=1, replica_groups=mesh['vocab'=8,'batch'=4] {'vocab'}, use_global_device_ids=true, to_apply=%region_3.4 | all-reduce | flops 64 | bytes 512 | tf_op jit(solution)/shard_map/pmax | solution.py:62
  65.5 0.3 fusion
  65.7 19.1 %all-reduce = (f32[64]{0:T(128)S(1)}, f32[64]{0:T(128)S(1)}) all-reduce(f32[64]{0:T(128)S(1)} %get-tuple-element.3, f32[64]{0:T(128)S(1)} %get-tuple-element.2), channel_id=1, replica_groups=mesh['vocab'=8,'batch'=4] {'vocab'}, use_global_device_ids=true, to_apply=%region_5.6 | all-reduce | flops 128 | bytes 1024 | tf_op jit(solution)/shard_map/psum | solution.py:66
  84.9 0.1 fusion.2
  85.0 0.7 copy.21
  85.7 3.3 %all-to-all-start = ((bf16[64,4,256]{2,0,1:T(8,128)(2,1)}), bf16[64,4,256]{2,0,1:T(8,128)(2,1)S(1)}, u32[]{:S(2)}, u32[]{:S(2)}) async-start(bf16[64,4,256]{2,0,1:T(8,128)(2,1)} %bitcast.32), calls=%async_computation | async-start | bytes 262144 | tf_op jit(solution)/shard_map/all_to_all | solution.py:76
  89.0 8.2 %all_gather.3 = bf16[256,1024]{1,0:T(8,128)(2,1)S(1)} all-gather(bf16[64,1024]{1,0:T(8,128)(2,1)S(1)} %constant_dynamic-update-slice_fusion), channel_id=1, replica_groups=mesh['vocab'=8,'batch'=4] {'batch'}, dimensions={0}, use_global_device_ids=true | all-gather | bytes 655360 | tf_op jit(solution)/shard_map/all_gather | solution.py:77
  97.3 0.6 dynamic_slice.8
  97.8 0.3 convolution_convert_fusion
  98.2 0.3 convolution_convert_fusion.1
  98.5 0.3 convolution_convert_fusion.2
  98.8 0.3 convolution_convert_fusion.3
  99.1 1.1 %add_convert_fusion = bf16[256,1024]{1,0:T(8,128)(2,1)} fusion(bf16[256,1024]{1,0:T(8,128)(2,1)S(1)} %convolution_convert_fusion, bf16[256,1024]{1,0:T(8,128)(2,1)S(1)} %convolution_convert_fusion.1, bf16[256,1024]{1,0:T(8,128)(2,1)S(1)} %convolution_convert_fusion.2, bf16[256,1024]{1,0:T(8,128)(2,1)S(1)} %convolution_convert_fusion.3), kind=kLoop, calls=%fused_computation.6 | loop fusion | flops 2097152 | bytes 2621440 | tf_op jit(solution)/shard_map/convert_element_type | solution.py:87
  (25 shorter events, 0.3 us)
Async XLA Ops:
  0.6 46.8 %copy-start = (bf16[1024,1024]{1,0:T(8,128)(2,1)S(1)}, bf16[1024,1024]{1,0:T(8,128)(2,1)}, u32[]{:S(2)}) copy-start(bf16[1024,1024]{1,0:T(8,128)(2,1)} %param.7) | copy-start | bytes 6291460
  0.6 8.0 %collective-permute-start = (bf16[8,1024]{1,0:T(8,128)(2,1)}, bf16[8,1024]{1,0:T(8,128)(2,1)S(1)}, u32[]{:S(2)}, u32[]{:S(2)}) collective-permute-start(bf16[8,1024]{1,0:T(8,128)(2,1)} %param.6), channel_id=1, source_target_pairs={{0,4},{4,8},{8,12},{12,16},{16,20},{20,24},{24,28},{28,0},{1,5},{5... | collective-permute-start | bytes 49160 | tf_op jit(solution)/shard_map/ppermute | solution.py:27
  8.6 6.4 %collective-permute-start.1 = (bf16[8,1024]{1,0:T(8,128)(2,1)S(1)}, bf16[8,1024]{1,0:T(8,128)(2,1)S(1)}, u32[]{:S(2)}, u32[]{:S(2)}) collective-permute-start(bf16[8,1024]{1,0:T(8,128)(2,1)S(1)} %collective-permute-done), channel_id=1, source_target_pairs={{0,4},{4,8},{8,12},{12,16},{16,20},{20,24},{24,28},{28,0},{1,5},{5... | collective-permute-start | bytes 49160 | tf_op jit(solution)/shard_map/ppermute | solution.py:27
  15.1 6.4 %collective-permute-start.2 = (bf16[8,1024]{1,0:T(8,128)(2,1)S(1)}, bf16[8,1024]{1,0:T(8,128)(2,1)S(1)}, u32[]{:S(2)}, u32[]{:S(2)}) collective-permute-start(bf16[8,1024]{1,0:T(8,128)(2,1)S(1)} %collective-permute-done.1), channel_id=1, source_target_pairs={{0,4},{4,8},{8,12},{12,16},{16,20},{20,24},{24,28},{28,0},{1,5},{5... | collective-permute-start | bytes 49160 | tf_op jit(solution)/shard_map/ppermute | solution.py:27
  21.5 6.4 %collective-permute-start.3 = (bf16[8,1024]{1,0:T(8,128)(2,1)S(1)}, bf16[8,1024]{1,0:T(8,128)(2,1)S(1)}, u32[]{:S(2)}, u32[]{:S(2)}) collective-permute-start(bf16[8,1024]{1,0:T(8,128)(2,1)S(1)} %collective-permute-done.2), channel_id=1, source_target_pairs={{0,4},{4,8},{8,12},{12,16},{16,20},{20,24},{24,28},{28,0},{1,5},{5... | collective-permute-start | bytes 49160 | tf_op jit(solution)/shard_map/ppermute | solution.py:27
  27.9 6.5 %collective-permute-start.4 = (bf16[8,1024]{1,0:T(8,128)(2,1)S(1)}, bf16[8,1024]{1,0:T(8,128)(2,1)S(1)}, u32[]{:S(2)}, u32[]{:S(2)}) collective-permute-start(bf16[8,1024]{1,0:T(8,128)(2,1)S(1)} %collective-permute-done.3), channel_id=1, source_target_pairs={{0,4},{4,8},{8,12},{12,16},{16,20},{20,24},{24,28},{28,0},{1,5},{5... | collective-permute-start | bytes 49160 | tf_op jit(solution)/shard_map/ppermute | solution.py:27
  34.5 6.4 %collective-permute-start.5 = (bf16[8,1024]{1,0:T(8,128)(2,1)S(1)}, bf16[8,1024]{1,0:T(8,128)(2,1)S(1)}, u32[]{:S(2)}, u32[]{:S(2)}) collective-permute-start(bf16[8,1024]{1,0:T(8,128)(2,1)S(1)} %collective-permute-done.4), channel_id=1, source_target_pairs={{0,4},{4,8},{8,12},{12,16},{16,20},{20,24},{24,28},{28,0},{1,5},{5... | collective-permute-start | bytes 49160 | tf_op jit(solution)/shard_map/ppermute | solution.py:27
  40.9 6.4 %collective-permute-start.6 = (bf16[8,1024]{1,0:T(8,128)(2,1)S(1)}, bf16[8,1024]{1,0:T(8,128)(2,1)S(1)}, u32[]{:S(2)}, u32[]{:S(2)}) collective-permute-start(bf16[8,1024]{1,0:T(8,128)(2,1)S(1)} %collective-permute-done.5), channel_id=1, source_target_pairs={{0,4},{4,8},{8,12},{12,16},{16,20},{20,24},{24,28},{28,0},{1,5},{5... | collective-permute-start | bytes 49160 | tf_op jit(solution)/shard_map/ppermute | solution.py:27
  85.7 12.2 %all-to-all-start = ((bf16[64,4,256]{2,0,1:T(8,128)(2,1)}), bf16[64,4,256]{2,0,1:T(8,128)(2,1)S(1)}, u32[]{:S(2)}, u32[]{:S(2)}) async-start(bf16[64,4,256]{2,0,1:T(8,128)(2,1)} %bitcast.32), calls=%async_computation | async-start | bytes 262144 | tf_op jit(solution)/shard_map/all_to_all | solution.py:76
